TPU v7x, 256 devices: a whole 4x4x8 slice. The times are simulated.
256 devices in a mesh: cells: 16 (over z, core), lev: 16 (over x, y).
Axes of the slice: x: 4, y: 4, z: 8, core: 2. Of those that a mesh axis runs over, the one named last changes fastest.
Arguments:
- source_levels: float32 [128, 65536], P('lev', 'cells'), may hold values from -6 to 6
- level_to_mode: float32 [128, 128], replicated, may hold values from -0.5 to 0.5
- mode_to_level: float32 [128, 128], replicated, may hold values from -0.5 to 0.5
- mode_shift: float32 [128], P('lev'), may hold values from 0.02 to 1
- edge_weight: float32 [6, 65536], P(None, 'cells'), may hold values from 0.05 to 0.5
- neighbours: int32 [6, 65536], P(None, 'cells'), may hold values from 0 to 6143, as said below
- send_lists: int32 [16, 2048], P('cells'), may hold values from 0 to 4095, as said below
Outputs:
- correction: float32 [128, 65536], P('lev', 'cells')
Inputs may be any that keep to these rules, and one draw needn't show every extreme that they name: `neighbours`: an entry below 4096 is a cell of the same partition whose local index differs from the cell's own local index by at most 32; an entry e of partition p at or above 4096 names halo slot h = (e - 4096) % 128 from partition s = (e - 4096) // 128, with s not p and h below the number of cells that s sends to p. An unused entry names the cell itself. `send_lists`: the number of used slots from partition s to partition q differs from pair to pair: 1 to 128 for every pair of different partitions, 0 for a partition and itself; in every draw some partition receives 128 cells from every other one. Unused slots hold any cell.
All inputs are finite; a program needn't handle non-finite values.
Results may differ from a plain program's by a relative error of at most 0.00007.
Values sent between devices are 32-bit elements; how exact they have to be, the bound alone decides.
A program may use at most 64 MiB of HBM per device.

v0:
```python
import jax
import jax.numpy as jnp
from jax import lax
from jax.sharding import PartitionSpec as P

DEG = 6
HMAX = 128
SWEEPS = 2
STEPS = 4


def full_product(left, right):
    return jnp.dot(left, right, precision=lax.Precision.HIGHEST, preferred_element_type=jnp.float32)


def local(
    source_levels, level_to_mode, mode_to_level, mode_shift, edge_weight, neighbours, send_lists
):
    slab_rows = source_levels.shape[0]
    position = lax.axis_index("lev")
    send_cells = send_lists.reshape(-1)
    slot_total = send_cells.shape[0]
    diagonal = jnp.sum(edge_weight, axis=0)
    own_rows = lax.dynamic_slice_in_dim(level_to_mode, position * slab_rows, slab_rows, 0)
    mode_field = full_product(own_rows, lax.all_gather(source_levels, "lev", axis=0, tiled=True))
    shift_col = mode_shift[:, None]
    own_scale = shift_col + diagonal[None, :]

    def apply_operator(field):
        outgoing = jnp.take(field, send_cells, axis=1)
        arrived = lax.all_to_all(
            outgoing.reshape(slab_rows, -1, HMAX), "cells", split_axis=1, concat_axis=1, tiled=True
        ).reshape(slab_rows, slot_total)
        extended = jnp.concatenate([field, arrived], axis=1)
        running = own_scale * field
        for slot_number in range(DEG):
            running = running - edge_weight[slot_number][None, :] * jnp.take(
                extended, neighbours[slot_number], axis=1
            )
        return running

    radius = DEG / 2.0
    centre = shift_col + radius
    sigma_ratio = centre / radius
    answer = jnp.zeros_like(mode_field)
    remain = mode_field
    direction = jnp.zeros_like(mode_field)
    factor = 1.0 / sigma_ratio
    for sweep_index in range(SWEEPS):
        for step_index in range(STEPS):
            if step_index == 0:
                if sweep_index > 0:
                    remain = remain - apply_operator(direction)
                factor = 1.0 / sigma_ratio
                direction = remain / centre
            else:
                remain = remain - apply_operator(direction)
                newer = 1.0 / (2.0 * sigma_ratio - factor)
                direction = newer * factor * direction + 2.0 * newer / radius * remain
                factor = newer
            answer = answer + direction
    own_columns = lax.dynamic_slice_in_dim(mode_to_level, position * slab_rows, slab_rows, 1)
    return lax.psum_scatter(
        full_product(own_columns, answer), "lev", scatter_dimension=0, tiled=True
    )


def solution(mesh):
    in_specs = (
        P("lev", "cells"),
        P(),
        P(),
        P("lev"),
        P(None, "cells"),
        P(None, "cells"),
        P("cells", None),
    )
    out_specs = P("lev", "cells")
    return jax.shard_map(local, mesh=mesh, in_specs=in_specs, out_specs=out_specs, check_vma=False)
```

profile of v0, /device:TPU:1, one launch (start us, length us, event | category | flops | bytes accessed | tf_op | source)
XLA Modules:
  0.0 1055.4 jit_solution(7952593365196662498)
XLA Ops:
  21.0 41.8 %all-gather.2.cloned.1.call-done = f32[128,4096]{1,0:T(8,128)} async-done(((f32[8,4096]{1,0:T(8,128)}), f32[128,4096]{1,0:T(8,128)}) %all-gather.2.cloned.1.call-update) | async-done | bytes 2097168 | tf_op jit(solution)/shard_map/all_gather | solution.py:25
  93.4 15.4 %gather_fusion.6 = f32[4096,8]{1,0:T(8,128)} fusion(f32[8,6144]{0,1:T(8,128)S(1)} %copy.108, s32[4096]{0:T(1024)} %fusion.90), kind=kCustom, calls=%fused_computation.12.clone | custom fusion | bytes 278528 | tf_op jit(solution)/shard_map/jit(_take)/gather | solution.py:37
  111.6 14.1 %gather_fusion.5 = f32[4096,8]{1,0:T(8,128)} fusion(f32[8,6144]{0,1:T(8,128)S(1)} %copy.108, s32[4096]{0:T(1024)S(1)} %copy-done.49), kind=kCustom, calls=%fused_computation.11.clone | custom fusion | bytes 278528 | tf_op jit(solution)/shard_map/jit(_take)/gather | solution.py:37
  128.5 14.1 %gather_fusion.4 = f32[4096,8]{1,0:T(8,128)} fusion(f32[8,6144]{0,1:T(8,128)S(1)} %copy.108, s32[4096]{0:T(1024)S(1)} %copy-done.47), kind=kCustom, calls=%fused_computation.10.clone | custom fusion | bytes 278528 | tf_op jit(solution)/shard_map/jit(_take)/gather | solution.py:37
  145.4 14.1 %gather_fusion.3 = f32[4096,8]{1,0:T(8,128)} fusion(f32[8,6144]{0,1:T(8,128)S(1)} %copy.108, s32[4096]{0:T(1024)S(1)} %copy-done.45), kind=kCustom, calls=%fused_computation.9.clone | custom fusion | bytes 278528 | tf_op jit(solution)/shard_map/jit(_take)/gather | solution.py:37
  162.4 14.1 %gather_fusion.2 = f32[4096,8]{1,0:T(8,128)} fusion(f32[8,6144]{0,1:T(8,128)S(1)} %copy.108, s32[4096]{0:T(1024)S(1)} %copy-done.41), kind=kCustom, calls=%fused_computation.8.clone | custom fusion | bytes 278528 | tf_op jit(solution)/shard_map/jit(_take)/gather | solution.py:37
  179.3 14.1 %gather_fusion.1 = f32[4096,8]{1,0:T(8,128)} fusion(f32[8,6144]{0,1:T(8,128)S(1)} %copy.108, s32[4096]{0:T(1024)S(1)} %copy-done.43), kind=kCustom, calls=%fused_computation.1.clone | custom fusion | bytes 278528 | tf_op jit(solution)/shard_map/jit(_take)/gather | solution.py:37
  205.3 10.5 all_to_all.35
  218.4 14.1 %gather_fusion.13 = f32[4096,8]{1,0:T(8,128)} fusion(f32[8,6144]{0,1:T(8,128)S(1)} %copy.122, s32[4096]{0:T(1024)S(1)} %copy-done.51), kind=kCustom, calls=%fused_computation.18.clone | custom fusion | bytes 278528 | tf_op jit(solution)/shard_map/jit(_take)/gather | solution.py:37
  232.5 14.1 %gather_fusion.12 = f32[4096,8]{1,0:T(8,128)} fusion(f32[8,6144]{0,1:T(8,128)S(1)} %copy.122, s32[4096]{0:T(1024)S(1)} %copy-done.50), kind=kCustom, calls=%fused_computation.17.clone | custom fusion | bytes 278528 | tf_op jit(solution)/shard_map/jit(_take)/gather | solution.py:37
  246.6 14.1 %gather_fusion.11 = f32[4096,8]{1,0:T(8,128)} fusion(f32[8,6144]{0,1:T(8,128)S(1)} %copy.122, s32[4096]{0:T(1024)S(1)} %copy-done.48), kind=kCustom, calls=%fused_computation.16.clone | custom fusion | bytes 278528 | tf_op jit(solution)/shard_map/jit(_take)/gather | solution.py:37
  260.7 14.1 %gather_fusion.10 = f32[4096,8]{1,0:T(8,128)} fusion(f32[8,6144]{0,1:T(8,128)S(1)} %copy.122, s32[4096]{0:T(1024)S(1)} %copy-done.46), kind=kCustom, calls=%fused_computation.15.clone | custom fusion | bytes 278528 | tf_op jit(solution)/shard_map/jit(_take)/gather | solution.py:37
  274.8 14.1 %gather_fusion.9 = f32[4096,8]{1,0:T(8,128)} fusion(f32[8,6144]{0,1:T(8,128)S(1)} %copy.122, s32[4096]{0:T(1024)S(1)} %copy-done.42), kind=kCustom, calls=%fused_computation.14.clone | custom fusion | bytes 278528 | tf_op jit(solution)/shard_map/jit(_take)/gather | solution.py:37
  288.9 14.1 %gather_fusion.8 = f32[4096,8]{1,0:T(8,128)} fusion(f32[8,6144]{0,1:T(8,128)S(1)} %copy.122, s32[4096]{0:T(1024)S(1)} %copy-done.44), kind=kCustom, calls=%fused_computation.13.clone | custom fusion | bytes 278528 | tf_op jit(solution)/shard_map/jit(_take)/gather | solution.py:37
  337.2 15.4 %gather_fusion.20 = f32[4096,8]{1,0:T(8,128)} fusion(f32[8,6144]{0,1:T(8,128)S(1)} %copy.136, s32[4096]{0:T(1024)} %fusion.90), kind=kCustom, calls=%fused_computation.24.clone | custom fusion | bytes 278528 | tf_op jit(solution)/shard_map/jit(_take)/gather | solution.py:37
  352.6 15.4 %gather_fusion.19 = f32[4096,8]{1,0:T(8,128)} fusion(f32[8,6144]{0,1:T(8,128)S(1)} %copy.136, s32[4096]{0:T(1024)} %fusion.89), kind=kCustom, calls=%fused_computation.23.clone | custom fusion | bytes 278528 | tf_op jit(solution)/shard_map/jit(_take)/gather | solution.py:37
  368.0 15.4 %gather_fusion.18 = f32[4096,8]{1,0:T(8,128)} fusion(f32[8,6144]{0,1:T(8,128)S(1)} %copy.136, s32[4096]{0:T(1024)} %fusion.88), kind=kCustom, calls=%fused_computation.22.clone | custom fusion | bytes 278528 | tf_op jit(solution)/shard_map/jit(_take)/gather | solution.py:37
  383.5 15.4 %gather_fusion.17 = f32[4096,8]{1,0:T(8,128)} fusion(f32[8,6144]{0,1:T(8,128)S(1)} %copy.136, s32[4096]{0:T(1024)} %fusion.87), kind=kCustom, calls=%fused_computation.21.clone | custom fusion | bytes 278528 | tf_op jit(solution)/shard_map/jit(_take)/gather | solution.py:37
  398.9 15.4 %gather_fusion.16 = f32[4096,8]{1,0:T(8,128)} fusion(f32[8,6144]{0,1:T(8,128)S(1)} %copy.136, s32[4096]{0:T(1024)} %fusion.86), kind=kCustom, calls=%fused_computation.20.clone | custom fusion | bytes 278528 | tf_op jit(solution)/shard_map/jit(_take)/gather | solution.py:37
  414.3 15.4 %gather_fusion.15 = f32[4096,8]{1,0:T(8,128)} fusion(f32[8,6144]{0,1:T(8,128)S(1)} %copy.136, s32[4096]{0:T(1024)} %fusion.85), kind=kCustom, calls=%fused_computation.19.clone | custom fusion | bytes 278528 | tf_op jit(solution)/shard_map/jit(_take)/gather | solution.py:37
  452.6 10.4 all_to_all.36
  465.5 15.4 %gather_fusion.27 = f32[4096,8]{1,0:T(8,128)} fusion(f32[8,6144]{0,1:T(8,128)S(1)} %copy.150, s32[4096]{0:T(1024)} %fusion.90), kind=kCustom, calls=%fused_computation.30.clone | custom fusion | bytes 278528 | tf_op jit(solution)/shard_map/jit(_take)/gather | solution.py:37
  480.9 15.4 %gather_fusion.26 = f32[4096,8]{1,0:T(8,128)} fusion(f32[8,6144]{0,1:T(8,128)S(1)} %copy.150, s32[4096]{0:T(1024)} %fusion.89), kind=kCustom, calls=%fused_computation.29.clone | custom fusion | bytes 278528 | tf_op jit(solution)/shard_map/jit(_take)/gather | solution.py:37
  496.3 15.4 %gather_fusion.25 = f32[4096,8]{1,0:T(8,128)} fusion(f32[8,6144]{0,1:T(8,128)S(1)} %copy.150, s32[4096]{0:T(1024)} %fusion.88), kind=kCustom, calls=%fused_computation.28.clone | custom fusion | bytes 278528 | tf_op jit(solution)/shard_map/jit(_take)/gather | solution.py:37
  511.7 15.4 %gather_fusion.24 = f32[4096,8]{1,0:T(8,128)} fusion(f32[8,6144]{0,1:T(8,128)S(1)} %copy.150, s32[4096]{0:T(1024)} %fusion.87), kind=kCustom, calls=%fused_computation.27.clone | custom fusion | bytes 278528 | tf_op jit(solution)/shard_map/jit(_take)/gather | solution.py:37
  527.1 15.4 %gather_fusion.23 = f32[4096,8]{1,0:T(8,128)} fusion(f32[8,6144]{0,1:T(8,128)S(1)} %copy.150, s32[4096]{0:T(1024)} %fusion.86), kind=kCustom, calls=%fused_computation.26.clone | custom fusion | bytes 278528 | tf_op jit(solution)/shard_map/jit(_take)/gather | solution.py:37
  542.6 15.4 %gather_fusion.22 = f32[4096,8]{1,0:T(8,128)} fusion(f32[8,6144]{0,1:T(8,128)S(1)} %copy.150, s32[4096]{0:T(1024)} %fusion.85), kind=kCustom, calls=%fused_computation.25.clone | custom fusion | bytes 278528 | tf_op jit(solution)/shard_map/jit(_take)/gather | solution.py:37
  579.8 10.4 all_to_all.37
  592.7 15.4 %gather_fusion.34 = f32[4096,8]{1,0:T(8,128)} fusion(f32[8,6144]{0,1:T(8,128)S(1)} %copy.164, s32[4096]{0:T(1024)} %fusion.90), kind=kCustom, calls=%fused_computation.36.clone | custom fusion | bytes 278528 | tf_op jit(solution)/shard_map/jit(_take)/gather | solution.py:37
  608.2 15.4 %gather_fusion.33 = f32[4096,8]{1,0:T(8,128)} fusion(f32[8,6144]{0,1:T(8,128)S(1)} %copy.164, s32[4096]{0:T(1024)} %fusion.89), kind=kCustom, calls=%fused_computation.35.clone | custom fusion | bytes 278528 | tf_op jit(solution)/shard_map/jit(_take)/gather | solution.py:37
  623.6 15.4 %gather_fusion.32 = f32[4096,8]{1,0:T(8,128)} fusion(f32[8,6144]{0,1:T(8,128)S(1)} %copy.164, s32[4096]{0:T(1024)} %fusion.88), kind=kCustom, calls=%fused_computation.34.clone | custom fusion | bytes 278528 | tf_op jit(solution)/shard_map/jit(_take)/gather | solution.py:37
  639.0 15.4 %gather_fusion.31 = f32[4096,8]{1,0:T(8,128)} fusion(f32[8,6144]{0,1:T(8,128)S(1)} %copy.164, s32[4096]{0:T(1024)} %fusion.87), kind=kCustom, calls=%fused_computation.33.clone | custom fusion | bytes 278528 | tf_op jit(solution)/shard_map/jit(_take)/gather | solution.py:37
  654.4 15.4 %gather_fusion.30 = f32[4096,8]{1,0:T(8,128)} fusion(f32[8,6144]{0,1:T(8,128)S(1)} %copy.164, s32[4096]{0:T(1024)} %fusion.86), kind=kCustom, calls=%fused_computation.32.clone | custom fusion | bytes 278528 | tf_op jit(solution)/shard_map/jit(_take)/gather | solution.py:37
  669.8 15.4 %gather_fusion.29 = f32[4096,8]{1,0:T(8,128)} fusion(f32[8,6144]{0,1:T(8,128)S(1)} %copy.164, s32[4096]{0:T(1024)} %fusion.85), kind=kCustom, calls=%fused_computation.31.clone | custom fusion | bytes 278528 | tf_op jit(solution)/shard_map/jit(_take)/gather | solution.py:37
  719.4 15.4 %gather_fusion.41 = f32[4096,8]{1,0:T(8,128)} fusion(f32[8,6144]{0,1:T(8,128)S(1)} %copy.178, s32[4096]{0:T(1024)} %fusion.90), kind=kCustom, calls=%fused_computation.42.clone | custom fusion | bytes 278528 | tf_op jit(solution)/shard_map/jit(_take)/gather | solution.py:37
  734.8 15.4 %gather_fusion.40 = f32[4096,8]{1,0:T(8,128)} fusion(f32[8,6144]{0,1:T(8,128)S(1)} %copy.178, s32[4096]{0:T(1024)} %fusion.89), kind=kCustom, calls=%fused_computation.41.clone | custom fusion | bytes 278528 | tf_op jit(solution)/shard_map/jit(_take)/gather | solution.py:37
  750.2 15.4 %gather_fusion.39 = f32[4096,8]{1,0:T(8,128)} fusion(f32[8,6144]{0,1:T(8,128)S(1)} %copy.178, s32[4096]{0:T(1024)} %fusion.88), kind=kCustom, calls=%fused_computation.40.clone | custom fusion | bytes 278528 | tf_op jit(solution)/shard_map/jit(_take)/gather | solution.py:37
  765.7 15.4 %gather_fusion.38 = f32[4096,8]{1,0:T(8,128)} fusion(f32[8,6144]{0,1:T(8,128)S(1)} %copy.178, s32[4096]{0:T(1024)} %fusion.87), kind=kCustom, calls=%fused_computation.39.clone | custom fusion | bytes 278528 | tf_op jit(solution)/shard_map/jit(_take)/gather | solution.py:37
  781.1 15.4 %gather_fusion.37 = f32[4096,8]{1,0:T(8,128)} fusion(f32[8,6144]{0,1:T(8,128)S(1)} %copy.178, s32[4096]{0:T(1024)} %fusion.86), kind=kCustom, calls=%fused_computation.38.clone | custom fusion | bytes 278528 | tf_op jit(solution)/shard_map/jit(_take)/gather | solution.py:37
  796.5 15.4 %gather_fusion.36 = f32[4096,8]{1,0:T(8,128)} fusion(f32[8,6144]{0,1:T(8,128)S(1)} %copy.178, s32[4096]{0:T(1024)} %fusion.85), kind=kCustom, calls=%fused_computation.37.clone | custom fusion | bytes 278528 | tf_op jit(solution)/shard_map/jit(_take)/gather | solution.py:37
  833.8 10.4 all_to_all.39
  846.7 15.4 %gather_fusion.48 = f32[4096,8]{1,0:T(8,128)} fusion(f32[8,6144]{0,1:T(8,128)S(1)} %copy.192, s32[4096]{0:T(1024)} %fusion.90), kind=kCustom, calls=%fused_computation.48.clone | custom fusion | bytes 278528 | tf_op jit(solution)/shard_map/jit(_take)/gather | solution.py:37
  862.2 15.4 %gather_fusion.47 = f32[4096,8]{1,0:T(8,128)} fusion(f32[8,6144]{0,1:T(8,128)S(1)} %copy.192, s32[4096]{0:T(1024)} %fusion.89), kind=kCustom, calls=%fused_computation.47.clone | custom fusion | bytes 278528 | tf_op jit(solution)/shard_map/jit(_take)/gather | solution.py:37
  877.6 15.4 %gather_fusion.46 = f32[4096,8]{1,0:T(8,128)} fusion(f32[8,6144]{0,1:T(8,128)S(1)} %copy.192, s32[4096]{0:T(1024)} %fusion.88), kind=kCustom, calls=%fused_computation.46.clone | custom fusion | bytes 278528 | tf_op jit(solution)/shard_map/jit(_take)/gather | solution.py:37
  893.0 15.4 %gather_fusion.45 = f32[4096,8]{1,0:T(8,128)} fusion(f32[8,6144]{0,1:T(8,128)S(1)} %copy.192, s32[4096]{0:T(1024)} %fusion.87), kind=kCustom, calls=%fused_computation.45.clone | custom fusion | bytes 278528 | tf_op jit(solution)/shard_map/jit(_take)/gather | solution.py:37
  908.4 15.4 %gather_fusion.44 = f32[4096,8]{1,0:T(8,128)} fusion(f32[8,6144]{0,1:T(8,128)S(1)} %copy.192, s32[4096]{0:T(1024)} %fusion.86), kind=kCustom, calls=%fused_computation.44.clone | custom fusion | bytes 278528 | tf_op jit(solution)/shard_map/jit(_take)/gather | solution.py:37
  923.8 15.4 %gather_fusion.43 = f32[4096,8]{1,0:T(8,128)} fusion(f32[8,6144]{0,1:T(8,128)S(1)} %copy.192, s32[4096]{0:T(1024)} %fusion.85), kind=kCustom, calls=%fused_computation.43.clone | custom fusion | bytes 278528 | tf_op jit(solution)/shard_map/jit(_take)/gather | solution.py:37
  954.5 92.5 %all-reduce.3.cloned.1.call-done = f32[128,4096]{1,0:T(8,128)} async-done(((f32[128,4096]{1,0:T(8,128)}), f32[128,4096]{1,0:T(8,128)}) %all-reduce.3.cloned.1.call-update) | async-done | bytes 2097168
  (398 shorter events, 230.6 us)
Async XLA Ops:
  6.5 943.2 %copy-start = (f32[128,128]{1,0:T(8,128)S(1)}, f32[128,128]{1,0:T(8,128)}, u32[]{:S(2)}) copy-start(f32[128,128]{1,0:T(8,128)} %param.13) | copy-start | bytes 196612
  6.5 56.2 %all-gather.2.cloned.1.call-start = ((), (), s32[]{:S(2)}) async-start(), calls=%async_computation.7 | async-start | bytes 2228224 | tf_op jit(solution)/shard_map/all_gather | solution.py:25
  11.1 54.3 %copy-start.115 = (f32[8]{0:T(128)}, f32[8]{0:T(128)S(1)}, u32[]{:S(2)}) copy-start(f32[8]{0:T(128)S(1)} %get-tuple-element.40) | copy-start | bytes 100
  65.4 130.4 %copy-start.19 = (f32[8,4096]{1,0:T(8,128)}, f32[8,4096]{1,0:T(8,128)S(1)}, u32[]{:S(2)}) copy-start(f32[8,4096]{1,0:T(8,128)S(1)} %get-tuple-element.42) | copy-start | bytes 393220
  72.5 10.5 copy-start.134
  72.5 10.5 copy-start.135
  72.5 10.5 copy-start.136
  74.5 16.3 %all-to-all-start = ((f32[8,16,128]{2,0,1:T(8,128)}), f32[8,16,128]{2,0,1:T(8,128)S(1)}, u32[]{:S(2)}, u32[]{:S(2)}) async-start(f32[8,16,128]{2,0,1:T(8,128)} %copy.107), calls=%async_computation | async-start | bytes 131072 | tf_op jit(solution)/shard_map/all_to_all | solution.py:31
  93.4 18.3 %copy-start.49 = (s32[4096]{0:T(1024)S(1)}, s32[4096]{0:T(1024)}, u32[]{:S(2)}) copy-start(s32[4096]{0:T(1024)} %fusion.89) | copy-start | bytes 49156
  111.6 16.9 %copy-start.47 = (s32[4096]{0:T(1024)S(1)}, s32[4096]{0:T(1024)}, u32[]{:S(2)}) copy-start(s32[4096]{0:T(1024)} %fusion.88) | copy-start | bytes 49156
  128.5 16.9 %copy-start.45 = (s32[4096]{0:T(1024)S(1)}, s32[4096]{0:T(1024)}, u32[]{:S(2)}) copy-start(s32[4096]{0:T(1024)} %fusion.87) | copy-start | bytes 49156
  145.4 16.9 %copy-start.41 = (s32[4096]{0:T(1024)S(1)}, s32[4096]{0:T(1024)}, u32[]{:S(2)}) copy-start(s32[4096]{0:T(1024)} %fusion.86) | copy-start | bytes 49156
  162.4 16.9 %copy-start.43 = (s32[4096]{0:T(1024)S(1)}, s32[4096]{0:T(1024)}, u32[]{:S(2)}) copy-start(s32[4096]{0:T(1024)} %fusion.85) | copy-start | bytes 49156
  205.3 13.1 %copy-start.51 = (s32[4096]{0:T(1024)S(1)}, s32[4096]{0:T(1024)}, u32[]{:S(2)}) copy-start(s32[4096]{0:T(1024)} %fusion.90) | copy-start | bytes 49156
  216.5 16.0 %copy-start.50 = (s32[4096]{0:T(1024)S(1)}, s32[4096]{0:T(1024)}, u32[]{:S(2)}) copy-start(s32[4096]{0:T(1024)} %fusion.89) | copy-start | bytes 49156
  216.5 30.1 %copy-start.48 = (s32[4096]{0:T(1024)S(1)}, s32[4096]{0:T(1024)}, u32[]{:S(2)}) copy-start(s32[4096]{0:T(1024)} %fusion.88) | copy-start | bytes 49156
  218.4 42.4 %copy-start.46 = (s32[4096]{0:T(1024)S(1)}, s32[4096]{0:T(1024)}, u32[]{:S(2)}) copy-start(s32[4096]{0:T(1024)} %fusion.87) | copy-start | bytes 49156
  218.4 56.4 %copy-start.42 = (s32[4096]{0:T(1024)S(1)}, s32[4096]{0:T(1024)}, u32[]{:S(2)}) copy-start(s32[4096]{0:T(1024)} %fusion.86) | copy-start | bytes 49156
  232.5 56.4 %copy-start.44 = (s32[4096]{0:T(1024)S(1)}, s32[4096]{0:T(1024)}, u32[]{:S(2)}) copy-start(s32[4096]{0:T(1024)} %fusion.85) | copy-start | bytes 49156
  321.3 5.6 copy-start.137
  323.2 11.4 %all-to-all-start.2 = ((f32[8,16,128]{2,0,1:T(8,128)}), f32[8,16,128]{2,0,1:T(8,128)S(1)}, u32[]{:S(2)}, u32[]{:S(2)}) async-start(f32[8,16,128]{2,0,1:T(8,128)} %copy.135), calls=%async_computation.2 | async-start | bytes 131072 | tf_op jit(solution)/shard_map/all_to_all | solution.py:31
  326.8 720.1 %all-reduce.3.cloned.1.call-start = ((), (), s32[]{:S(2)}) async-start(), calls=%async_computation.8 | async-start | bytes 4194304
  440.7 10.0 copy-start.106
  442.5 20.4 %copy-start.1 = (f32[8,4096]{1,0:T(8,128)}, f32[8,4096]{1,0:T(8,128)S(1)}, u32[]{:S(2)}) copy-start(f32[8,4096]{1,0:T(8,128)S(1)} %get-tuple-element.13) | copy-start | bytes 393220
  578.5 11.7 %copy-start.26 = (f32[8,4096]{1,0:T(8,128)S(1)}, f32[8,4096]{1,0:T(8,128)}, u32[]{:S(2)}) copy-start(f32[8,4096]{1,0:T(8,128)} %copy-done.25) | copy-start | bytes 393220
  695.5 9.2 copy-start.107
  696.5 20.4 %copy-start.4 = (f32[8,4096]{1,0:T(8,128)}, f32[8,4096]{1,0:T(8,128)S(1)}, u32[]{:S(2)}) copy-start(f32[8,4096]{1,0:T(8,128)S(1)} %get-tuple-element.9) | copy-start | bytes 393220
  817.0 4.7 copy-start.13
  832.4 11.8 %copy-start.24 = (f32[8,4096]{1,0:T(8,128)S(1)}, f32[8,4096]{1,0:T(8,128)}, u32[]{:S(2)}) copy-start(f32[8,4096]{1,0:T(8,128)} %copy-done.23) | copy-start | bytes 393220
  945.0 4.7 copy-start.3
  945.0 4.7 copy-start.6
  945.0 4.7 copy-start.20
  945.0 4.7 copy-start.22
  945.0 4.7 copy-start.33
  945.0 4.7 copy-start.40
  945.1 4.7 copy-start.54
  945.1 4.7 copy-start.70
  945.1 4.7 copy-start.77
  945.1 4.7 copy-start.84
  945.1 4.7 copy-start.91
  945.1 4.7 copy-start.98
  945.1 4.7 copy-start.105
  945.1 4.7 copy-start.114
  945.1 4.7 copy-start.119
  945.2 4.7 copy-start.122
  945.2 4.7 copy-start.125
  945.2 4.7 copy-start.131
  945.2 4.7 copy-start.133
  (95 other events, 302.1 us)
Sparse Core Ops, SparseCore 0:
  9.8 52.8 all-gather.1
  953.3 93.5 all-reduce.2
where the time goes:
time: 1070 us; the launch traced here: 1060 us
  local copies, waits for them, and re-layouts  788 us (74%)
  waiting for transfers between devices  149 us (14%)
  blocking collectives  52 us (5%)
  other arithmetic  32.2 us (3%)
  between operations  15.8 us (1%)
  starting transfers between devices  12.2 us (1%)
    gather x84, local copies, waits for them, and re-layouts, apply_operator(): jnp.take(extended, neighbours[slot_number], axis=1)  712 us
    unnamed x3, waiting for transfers between devices  93.2 us
    all_to_all x5, blocking collectives, apply_operator(): lax.all_to_all(outgoing.reshape(slab_rows, -1, HMAX), 'cells', split_axis...  52 us
    gather x7, local copies, waits for them, and re-layouts, apply_operator(): outgoing = jnp.take(field, send_cells, axis=1)  47.4 us
    all_gather x1, waiting for transfers between devices, local(): lax.all_gather(source_levels, 'lev', axis=0, tiled=True)  41.8 us
  transfers between devices with their start and end apart: 4, of which 4 were waited for; matrix products, arithmetic and copies ran while one was open for 1% of the time, Pallas kernels for 0%

commit v1 on v0

v1 whole, which is shorter than its diff:
```python
import functools
import math

import jax
import jax.numpy as jnp
from jax import lax
from jax.experimental import pallas as pl
from jax.experimental.pallas import tpu as pltpu
from jax.sharding import PartitionSpec as P

DEG = 6
HMAX = 128
SWEEPS = 2
STEPS = 4
TERMS = SWEEPS * STEPS
RADIUS = DEG / 2.0
MESH = pl.DeviceIdType.MESH
GATHER = lax.GatherDimensionNumbers(
    offset_dims=(),
    collapsed_slice_dims=(1,),
    start_index_map=(1,),
    operand_batching_dims=(0,),
    start_indices_batching_dims=(0,),
)


def lane_gather(block, lanes):
    return lax.gather(
        block, lanes[..., None], GATHER, slice_sizes=(1, 1), mode=lax.GatherScatterMode.PROMISE_IN_BOUNDS
    )


def full_product(left, right):
    return jnp.dot(left, right, precision=lax.Precision.HIGHEST, preferred_element_type=jnp.float32)


def peers_of(chips):
    places, groups = [(0, 1)], [(0, 1)]
    for far in range(1, chips // 2 + 1):
        start = len(places)
        for step in sorted({far, chips - far}):
            places += [(step, 0), (step, 1)]
        groups.append((start, len(places)))
    return places, groups


def block(row):
    return jnp.broadcast_to(row, (8, 128))


def chebyshev_coefficients(shift):
    lane = lax.broadcasted_iota(jnp.int32, (8, 128), 1)
    up = jnp.where(lane == 0, 0.0, jnp.where(lane == 1, 1.0, 0.5))
    down = jnp.where(lane < TERMS, 0.5, 0.0)

    def operator(poly):
        scaled = up * pltpu.roll(poly, 1, 1) + down * pltpu.roll(poly, 127, 1)
        return centre * poly + RADIUS * scaled

    centre = shift + RADIUS
    sigma = centre / RADIUS
    answer = jnp.zeros((8, 128), jnp.float32)
    remain = jnp.where(lane == 0, 1.0, 0.0)
    direction = answer
    factor = 1.0 / sigma
    for sweep_index in range(SWEEPS):
        for step_index in range(STEPS):
            if sweep_index + step_index > 0:
                remain = remain - operator(direction)
            if step_index == 0:
                factor = 1.0 / sigma
                direction = remain / centre
            else:
                newer = 1.0 / (2.0 * sigma - factor)
                direction = newer * factor * direction + (2.0 * newer / RADIUS) * remain
                factor = newer
            answer = answer + direction
    return answer


def kernel(
    parts, slabs, group_rows, rounds_of,
    shift_ref, source_ref, l2m_ref, m2l_ref, weight_ref, near_ref, list_ref,
    out_ref, flag_ref,
    edge, weight, lane_a, weight_a, weight_b, own, halo_lane, halo_weight, pack,
    give_s, have_s, give_g, have_g, field, total, send, halo, flag_out, flag_in,
    sem_s, sem_g, sem_send, sem_recv, sem_flag,
):
    columns = source_ref.shape[1]
    tiles = columns // 128
    eighths = tiles // 8
    share = tiles // slabs
    part = lax.axis_index("cells")
    slab = lax.axis_index("lev")
    chips = parts // 2
    places, groups = peers_of(chips)
    count = len(places)
    chip, core = part // 2, part % 2
    inverse = [places.index(((chips - step) % chips, swap)) for step, swap in places]

    def partition_at(place):
        step, swap = places[place]
        return ((chip + step) % chips) * 2 + (core + swap) % 2

    barrier = pltpu.get_barrier_semaphore()
    for place in range(count):
        pl.semaphore_signal(barrier, inc=1, device_id={"cells": partition_at(place)}, device_id_type=MESH)
    for step in range(1, slabs):
        pl.semaphore_signal(barrier, inc=1, device_id={"lev": (slab + step) % slabs}, device_id_type=MESH)

    row = lax.broadcasted_iota(jnp.int32, (8, 128), 0)
    shift = jnp.zeros((8, 128), jnp.float32)
    for index in range(8):
        shift = jnp.where(row == index, shift_ref[index], shift)
    coefficients = chebyshev_coefficients(shift)
    for peer in range(slabs):
        for piece in range(share):
            at = (peer * share + piece) * 128
            give_s[peer, piece] = source_ref[:, at : at + 128]
        give_s[peer, share] = coefficients
    have_s[slab] = give_s[slab]

    pl.semaphore_wait(barrier, count + slabs - 1)

    order = sorted(range(1, slabs), key=lambda step: -(step * 7 % slabs))
    for step in order:
        peer = (slab + step) % slabs
        pltpu.make_async_remote_copy(
            src_ref=give_s.at[peer], dst_ref=have_s.at[slab], send_sem=sem_s.at[0], recv_sem=sem_s.at[1],
            device_id={"lev": peer}, device_id_type=MESH,
        ).start()

    for k in range(DEG):
        for tile in range(tiles):
            edge[k, tile // 8, tile % 8 : tile % 8 + 1, :] = near_ref[k : k + 1, tile * 128 : tile * 128 + 128]
            weight[k, tile // 8, tile % 8 : tile % 8 + 1, :] = weight_ref[k : k + 1, tile * 128 : tile * 128 + 128]
    for g in range(eighths):
        diagonal = jnp.zeros((8, 128), jnp.float32)
        for k in range(DEG):
            entry = edge[k, g]
            value = weight[k, g]
            diagonal = diagonal + value
            scaled = value * (-2.0 / RADIUS)
            inside = entry < columns
            here = (entry >> 7) == (row + 8 * g)
            lane_a[k, g] = entry & 127
            weight_a[k, g] = jnp.where(here, scaled, 0.0)
            weight_b[k, g] = jnp.where(inside, jnp.where(here, 0.0, scaled), 0.0)
            edge[k, g] = jnp.where(inside, -1, entry - columns)
            weight[k, g] = scaled
        own[g] = (diagonal - RADIUS) * (2.0 / RADIUS)
    for place in range(count):
        start = pl.multiple_of(partition_at(place) * HMAX, HMAX)
        pack[place] = block(list_ref[0:1, pl.ds(start, HMAX)])

    group_count = eighths // group_rows

    def build(place, most):
        pair = (place + 1) // 2
        step = jnp.where(pair % 2 == 1, (pair + 1) // 2, chips - pair // 2)
        step = jnp.where(pair == 0, 0, step)
        wanted = ((chip + step) % chips) * 2 + (core + (place + 1) % 2) % 2
        for group in range(group_count):
            seen = jnp.zeros((8, 128), jnp.int32)
            lanes = [jnp.zeros((8, 128), jnp.int32)] * rounds_of
            for g in range(group * group_rows, (group + 1) * group_rows):
                shares = [jnp.zeros((8, 128), jnp.float32)] * rounds_of
                for k in range(DEG):
                    entry = edge[k, g]
                    value = weight[k, g]
                    match = (entry >> 7) == wanted
                    number = jnp.where(match, seen, -1)
                    slot = entry & 127
                    for r in range(rounds_of):
                        take = number == r
                        lanes[r] = jnp.where(take, slot, lanes[r])
                        shares[r] = jnp.where(take, value, shares[r])
                    seen = jnp.where(match, seen + 1, seen)
                for r in range(rounds_of):
                    halo_weight[place, r, g] = shares[r]
            for r in range(rounds_of):
                halo_lane[place, r, group] = lanes[r]
            most = jnp.maximum(most, seen)
        return most

    most = lax.fori_loop(0, count, build, jnp.zeros((8, 128), jnp.int32))
    flag_out[...] = jnp.where(most > rounds_of, 1.0, 0.0)
    for place in reversed(range(count)):
        pltpu.make_async_remote_copy(
            src_ref=flag_out, dst_ref=flag_in.at[inverse[place]], send_sem=sem_flag.at[0], recv_sem=sem_flag.at[1],
            device_id={"cells": partition_at(place)}, device_id_type=MESH,
        ).start()

    def wait(ref, sem):
        pltpu.make_async_copy(ref, ref, sem).wait()

    wait(have_s.at[pl.ds(0, slabs - 1)], sem_s.at[1])
    levels = slabs * 8
    modes = [full_product(l2m_ref[...], have_s[:, piece].reshape(levels, 128)) for piece in range(share)]
    table = have_s[:, share].reshape(levels, 128)
    stages = ((0, 1), (1, 2), (2, TERMS))
    for stage, (low, high) in enumerate(stages):
        for term in range(low, high):
            scale = table[:, TERMS - 1 - term : TERMS - term]
            for piece in range(share):
                mixed = full_product(m2l_ref[...], modes[piece] * scale)
                for peer in range(slabs):
                    give_g[peer, term, piece] = mixed[peer * 8 : peer * 8 + 8]
        for step in order:
            peer = (slab + step) % slabs
            pltpu.make_async_remote_copy(
                src_ref=give_g.at[peer, pl.ds(low, high - low)],
                dst_ref=have_g.at[pl.ds(low, high - low), slab],
                send_sem=sem_g.at[0, stage], recv_sem=sem_g.at[1, stage],
                device_id={"lev": peer}, device_id_type=MESH,
            ).start()
        for term in range(low, high):
            have_g[term, slab] = give_g[slab, term]

    def wait_stage(stage):
        low, high = stages[stage]
        wait(have_g.at[pl.ds(low, high - low), pl.ds(0, slabs - 1)], sem_g.at[1, stage])

    wait_stage(0)
    for tile in range(tiles):
        field[0, tile] = have_g[0, tile // share, tile % share]
        field[1, tile] = jnp.zeros((8, 128), jnp.float32)

    half = lax.broadcasted_iota(jnp.int32, (8, 128), 1) < 64
    bits = int(math.log2(tiles))

    def application(turn, carry):
        now = turn % 2
        old = 1 - now

        @pl.when(turn >= 2)
        def _():
            wait(send.at[now], sem_send.at[now])

        for place in reversed(range(count)):
            code = pack[place]
            lanes = code & 127
            found = [lane_gather(field[now, tile], lanes) for tile in range(tiles)]
            for bit in range(bits):
                odd = (code & (128 << bit)) != 0
                found = [jnp.where(odd, found[2 * i + 1], found[2 * i]) for i in range(len(found) // 2)]
            send[now, place] = found[0]
            group = [i for i, (low, high) in enumerate(groups) if low <= inverse[place] < high][0]
            pltpu.make_async_remote_copy(
                src_ref=send.at[now, place], dst_ref=halo.at[now, inverse[place]],
                send_sem=sem_send.at[now], recv_sem=sem_recv.at[now, group],
                device_id={"cells": partition_at(place)}, device_id_type=MESH,
            ).start()

        for tile in range(tiles):
            g, t = tile // 8, tile % 8
            middle = field[now, tile]
            sides = jnp.where(half, field[now, min(tile + 1, tiles - 1)], field[now, max(tile - 1, 0)])
            value = middle * block(own[g, t : t + 1, :])
            for k in range(DEG):
                lanes = block(lane_a[k, g, t : t + 1, :])
                value = value + block(weight_a[k, g, t : t + 1, :]) * lane_gather(middle, lanes)
                value = value + block(weight_b[k, g, t : t + 1, :]) * lane_gather(sides, lanes)
            total[tile] = value

        @pl.when(turn == 0)
        def _():
            wait_stage(1)

        @pl.when(turn == 1)
        def _():
            wait_stage(2)

        scale = jnp.where(turn == TERMS - 2, 0.5, 1.0)
        for index, (low, high) in enumerate(groups):
            wait(halo.at[now, pl.ds(low, high - low)], sem_recv.at[now, index])
            for t in range(8):
                for group in range(group_count):
                    rows = range(group * group_rows, (group + 1) * group_rows)
                    values = [total[8 * g + t] for g in rows]
                    for place in range(low, high):
                        arrived = halo[now, place]
                        for r in range(rounds_of):
                            lanes = block(halo_lane[place, r, group, t : t + 1, :])
                            got = lane_gather(arrived, lanes)
                            for i, g in enumerate(rows):
                                values[i] = values[i] + block(halo_weight[place, r, g, t : t + 1, :]) * got
                    for i, g in enumerate(rows):
                        tile = 8 * g + t
                        if index < len(groups) - 1:
                            total[tile] = values[i]
                        else:
                            field[old, tile] = (
                                have_g[turn + 1, tile // share, tile % share] + scale * values[i] - field[old, tile]
                            )
        return carry

    lax.fori_loop(0, TERMS - 1, application, 0)

    last = (TERMS - 1) % 2
    for tile in range(tiles):
        out_ref[:, tile * 128 : tile * 128 + 128] = field[last, tile]

    for now in range(2):
        wait(send.at[now], sem_send.at[now])
    wait(give_s.at[pl.ds(0, slabs - 1)], sem_s.at[0])
    for stage, (low, high) in enumerate(stages):
        wait(have_g.at[pl.ds(low, high - low), pl.ds(0, slabs - 1)], sem_g.at[0, stage])
    wait(flag_in, sem_flag.at[0])
    wait(flag_in, sem_flag.at[1])
    worst = flag_out[...]
    for place in range(count):
        worst = jnp.maximum(worst, flag_in[place])
    flag_ref[...] = worst


def solve(parts, slabs, group_rows, rounds_of, number, source, l2m, m2l, shift, weights, near, lists):
    columns = source.shape[1]
    tiles = columns // 128
    eighths = tiles // 8
    share = tiles // slabs
    peers = parts - 1
    f32, i32 = jnp.float32, jnp.int32
    groups = len(peers_of(parts // 2)[1])
    vmem = pl.BlockSpec(memory_space=pltpu.VMEM)
    return pl.pallas_call(
        functools.partial(kernel, parts, slabs, group_rows, rounds_of),
        name=f"solve_{number}",
        out_shape=(
            jax.ShapeDtypeStruct(source.shape, f32),
            jax.ShapeDtypeStruct((8, 128), f32),
        ),
        in_specs=[pl.BlockSpec(memory_space=pltpu.SMEM)] + [vmem] * 6,
        out_specs=(vmem, vmem),
        scratch_shapes=[
            pltpu.VMEM((DEG, eighths, 8, 128), i32),
            pltpu.VMEM((DEG, eighths, 8, 128), f32),
            pltpu.VMEM((DEG, eighths, 8, 128), i32),
            pltpu.VMEM((DEG, eighths, 8, 128), f32),
            pltpu.VMEM((DEG, eighths, 8, 128), f32),
            pltpu.VMEM((eighths, 8, 128), f32),
            pltpu.VMEM((peers, rounds_of, eighths // group_rows, 8, 128), i32),
            pltpu.VMEM((peers, rounds_of, eighths, 8, 128), f32),
            pltpu.VMEM((peers, 8, 128), i32),
            pltpu.VMEM((slabs, share + 1, 8, 128), f32),
            pltpu.VMEM((slabs, share + 1, 8, 128), f32),
            pltpu.VMEM((slabs, TERMS, share, 8, 128), f32),
            pltpu.VMEM((TERMS, slabs, share, 8, 128), f32),
            pltpu.VMEM((2, tiles, 8, 128), f32),
            pltpu.VMEM((tiles, 8, 128), f32),
            pltpu.VMEM((2, peers, 8, 128), f32),
            pltpu.VMEM((2, peers, 8, 128), f32),
            pltpu.VMEM((8, 128), f32),
            pltpu.VMEM((peers, 8, 128), f32),
            pltpu.SemaphoreType.DMA((2,)),
            pltpu.SemaphoreType.DMA((2, 3)),
            pltpu.SemaphoreType.DMA((2,)),
            pltpu.SemaphoreType.DMA((2, groups)),
            pltpu.SemaphoreType.DMA((2,)),
        ],
        compiler_params=pltpu.CompilerParams(
            collective_id=number, has_side_effects=True, vmem_limit_bytes=40 << 20
        ),
    )(shift, source, l2m, m2l, weights, near, lists)


FAST = (4, 5)
SAFE = (1, DEG)


def solution(mesh):
    parts, slabs = mesh.shape["cells"], mesh.shape["lev"]

    def local(source, l2m, m2l, shift, weights, near, lists):
        arrays = (source, l2m, m2l, shift, weights, near, lists)
        eighths = source.shape[1] // 1024
        fast = (min(FAST[0], eighths), FAST[1])
        answer, flag = solve(parts, slabs, *fast, 0, *arrays)
        return lax.cond(
            flag[0, 0] > 0.0,
            lambda arrays, answer: solve(parts, slabs, *SAFE, 1, *arrays)[0],
            lambda arrays, answer: answer,
            arrays,
            answer,
        )

    in_specs = (P("lev", "cells"), P(), P(), P("lev"), P(None, "cells"), P(None, "cells"), P("cells", None))
    return jax.shard_map(local, mesh=mesh, in_specs=in_specs, out_specs=P("lev", "cells"), check_vma=False)
```

time: 1070 us -> 72.9 us (0.07); the launches traced: 1060 us -> 72.8 us
  local copies, waits for them, and re-layouts: 788 us -> 1.85 us
  waiting for transfers between devices: 149 us -> 0 us
  Pallas kernels: 0 us -> 70 us
  blocking collectives: 52 us -> 0 us
  other arithmetic: 32.2 us -> 0 us
  between operations: 15.8 us -> 0.74 us
  starting transfers between devices: 12.2 us -> 0 us
    gather x91 -> x0, local copies, waits for them, and re-layouts: 760 us -> none  [the longest x84 712 us: apply_operator(): jnp.take(extended, neighbours[slot_number], axis=1)]
    unnamed x3 -> x0, waiting for transfers between devices: 93.2 us -> none
    pallas_call x0 -> x1, Pallas kernels: none -> 70 us  [solve(): pl.pallas_call(functools.partial(kernel, parts, slabs, group_rows, rounds...]
    all_to_all x5 -> x0, blocking collectives: 52 us -> none  [apply_operator(): lax.all_to_all(outgoing.reshape(slab_rows, -1, HMAX), 'cells', split_axis...]
    all_gather x1 -> x0, waiting for transfers between devices: 41.8 us -> none  [local(): lax.all_gather(source_levels, 'lev', axis=0, tiled=True)]
    all_to_all x2 -> x0, waiting for transfers between devices: 14.4 us -> none  [apply_operator(): lax.all_to_all(outgoing.reshape(slab_rows, -1, HMAX), 'cells', split_axis...]
    concatenate x7 -> x0, local copies, waits for them, and re-layouts: 13 us -> none  [apply_operator(): extended = jnp.concatenate([field, arrived], axis=1)]
    all_to_all x2 -> x0, starting transfers between devices: 12.1 us -> none  [apply_operator(): lax.all_to_all(outgoing.reshape(slab_rows, -1, HMAX), 'cells', split_axis...]
  transfers between devices with their start and end apart: 4 -> 0, of which waited for: 4 -> 0; matrix products, arithmetic and copies ran while one was open for 1% -> 0% of each run, Pallas kernels for 0% -> 0%
where the time goes in v1:
time: 72.9 us; the launch traced here: 72.8 us
  Pallas kernels  70 us (96%)
  local copies, waits for them, and re-layouts  1.85 us (3%)
  between operations  0.74 us (1%)
    pallas_call x1, Pallas kernels, solve(): pl.pallas_call(functools.partial(kernel, parts, slabs, group_rows, rounds...  70 us

profile of v1, /device:TPU:1, one launch (start us, length us, event | category | flops | bytes accessed | tf_op | source)
XLA Modules:
  0.0 72.8 jit_solution(10577332772035814487)
XLA Ops:
  0.0 0.0 copy-start.6
  0.0 0.7 copy-done.6
  0.7 0.0 copy-start
  0.7 0.0 copy-start.1
  0.7 0.0 copy-start.2
  0.7 0.0 copy-start.3
  0.7 0.0 copy-start.4
  0.7 70.0 %solve_0.1 = (f32[8,4096]{1,0:T(8,128)S(1)}, f32[8,128]{1,0:T(8,128)S(1)}) custom-call(f32[8]{0:T(128)S(1)} %copy-done.6, f32[8,4096]{1,0:T(8,128)} %source_ref.1, f32[128,128]{1,0:T(8,128)} %l2m_ref.1, f32[128,128]{1,0:T(8,128)} %m2l_ref.1, f32[6,4096]{1,0:T(8,128)} %weight_ref.1, s32[6,4096]{1,0:T(8,128)} %near_ref.1, s32[1,2048]{1,0:T(1,128)} %list_ref.1), custom_call_target="tpu_custom_call" | custom-call | tf_op jit(solution)/shard_map/solve_0/pallas_call | solution.py:326
  70.7 0.0 copy-start.5
  70.7 0.5 slice.3
  71.9 0.0 copy-done
  71.9 0.0 copy-done.1
  71.9 0.0 copy-done.2
  71.9 0.0 copy-done.3
  71.9 0.0 copy-done.4
  71.9 0.0 copy-done.5
  71.9 0.2 conditional.1
  72.1 0.7 copy.13
Async XLA Ops:
  0.0 0.7 copy-start.6
  0.7 71.2 %copy-start = (f32[8,4096]{1,0:T(8,128)S(1)}, f32[8,4096]{1,0:T(8,128)}, u32[]{:S(2)}) copy-start(f32[8,4096]{1,0:T(8,128)} %source_ref.1) | copy-start | bytes 393220
  0.7 71.2 %copy-start.1 = (f32[6,4096]{1,0:T(8,128)S(1)}, f32[6,4096]{1,0:T(8,128)}, u32[]{:S(2)}) copy-start(f32[6,4096]{1,0:T(8,128)} %weight_ref.1) | copy-start | bytes 294916
  0.7 71.2 %copy-start.2 = (s32[6,4096]{1,0:T(8,128)S(1)}, s32[6,4096]{1,0:T(8,128)}, u32[]{:S(2)}) copy-start(s32[6,4096]{1,0:T(8,128)} %near_ref.1) | copy-start | bytes 294916
  0.7 71.2 %copy-start.3 = (f32[128,128]{1,0:T(8,128)S(1)}, f32[128,128]{1,0:T(8,128)}, u32[]{:S(2)}) copy-start(f32[128,128]{1,0:T(8,128)} %l2m_ref.1) | copy-start | bytes 196612
  0.7 71.2 %copy-start.4 = (f32[128,128]{1,0:T(8,128)S(1)}, f32[128,128]{1,0:T(8,128)}, u32[]{:S(2)}) copy-start(f32[128,128]{1,0:T(8,128)} %m2l_ref.1) | copy-start | bytes 196612
  70.7 1.2 %copy-start.5 = (s32[1,2048]{1,0:T(1,128)S(1)}, s32[1,2048]{1,0:T(1,128)}, u32[]{:S(2)}) copy-start(s32[1,2048]{1,0:T(1,128)} %list_ref.1) | copy-start | bytes 24580

commit v2 on v1

--- a/solution.py
+++ b/solution.py
@@ -42,6 +42,17 @@
             places += [(step, 0), (step, 1)]
         groups.append((start, len(places)))
     return places, groups
+
+
+def far_first(slabs):
+    side = math.isqrt(slabs)
+
+    def hops(step):
+        along, across = step // side, step % side
+        rows = -(-slabs // side)
+        return min(along, rows - along) + min(across, side - across)
+
+    return sorted(range(1, slabs), key=lambda step: -hops(step))
 
 
 def block(row):
@@ -79,13 +90,25 @@
 
 
 def kernel(
-    parts, slabs, group_rows, rounds_of,
+    parts, slabs, group_rows, rounds_of, spare,
+    shift_hbm, source_hbm, l2m_hbm, m2l_hbm, weight_hbm, near_hbm, list_hbm,
+    out_ref, flag_ref,
     shift_ref, source_ref, l2m_ref, m2l_ref, weight_ref, near_ref, list_ref,
-    out_ref, flag_ref,
-    edge, weight, lane_a, weight_a, weight_b, own, halo_lane, halo_weight, pack,
-    give_s, have_s, give_g, have_g, field, total, send, halo, flag_out, flag_in,
-    sem_s, sem_g, sem_send, sem_recv, sem_flag,
+    edge, weight, lane_a, weight_a, weight_b, own, halo_lane, halo_weight, extra_code, extra_weight, pack,
+    give_s, have_s, modes_ref, table_ref, give_g, have_g, field, total, send, halo, flag_out, flag_in,
+    sem_in, sem_s, sem_g, sem_send, sem_recv, sem_flag,
 ):
+    loads = [
+        pltpu.make_async_copy(far, near, sem_in.at[index])
+        for index, (far, near) in enumerate(
+            (
+                (shift_hbm, shift_ref), (source_hbm, source_ref), (near_hbm, near_ref), (weight_hbm, weight_ref),
+                (list_hbm, list_ref), (l2m_hbm, l2m_ref), (m2l_hbm, m2l_ref),
+            )
+        )
+    ]
+    for load in loads:
+        load.start()
     columns = source_ref.shape[1]
     tiles = columns // 128
     eighths = tiles // 8
@@ -103,16 +126,25 @@
         return ((chip + step) % chips) * 2 + (core + swap) % 2
 
     barrier = pltpu.get_barrier_semaphore()
-    for place in range(count):
+    order = far_first(slabs)
+    order2 = sorted(range(1, slabs), key=lambda step: -(step * 7 % slabs))
+    for place in reversed(range(count)):
         pl.semaphore_signal(barrier, inc=1, device_id={"cells": partition_at(place)}, device_id_type=MESH)
-    for step in range(1, slabs):
+        turn = count - 1 - place
+        if turn < slabs - 1:
+            peer = (slab + order[turn]) % slabs
+            pl.semaphore_signal(barrier, inc=1, device_id={"lev": peer}, device_id_type=MESH)
+    for step in order[count:]:
         pl.semaphore_signal(barrier, inc=1, device_id={"lev": (slab + step) % slabs}, device_id_type=MESH)
 
     row = lax.broadcasted_iota(jnp.int32, (8, 128), 0)
-    shift = jnp.zeros((8, 128), jnp.float32)
-    for index in range(8):
-        shift = jnp.where(row == index, shift_ref[index], shift)
+    loads[0].wait()
+    square = (8, 8)
+    diagonal = lax.broadcasted_iota(jnp.int32, square, 0) == lax.broadcasted_iota(jnp.int32, square, 1)
+    shift = jnp.where(diagonal, jnp.broadcast_to(shift_ref[...].reshape(1, 8), square), 0.0)
+    shift = jnp.broadcast_to(jnp.sum(shift, axis=1, keepdims=True), (8, 128))
     coefficients = chebyshev_coefficients(shift)
+    loads[1].wait()
     for peer in range(slabs):
         for piece in range(share):
             at = (peer * share + piece) * 128
@@ -122,7 +154,6 @@
 
     pl.semaphore_wait(barrier, count + slabs - 1)
 
-    order = sorted(range(1, slabs), key=lambda step: -(step * 7 % slabs))
     for step in order:
         peer = (slab + step) % slabs
         pltpu.make_async_remote_copy(
@@ -130,6 +161,8 @@
             device_id={"lev": peer}, device_id_type=MESH,
         ).start()
 
+    for load in loads[2:5]:
+        load.wait()
     for k in range(DEG):
         for tile in range(tiles):
             edge[k, tile // 8, tile % 8 : tile % 8 + 1, :] = near_ref[k : k + 1, tile * 128 : tile * 128 + 128]
@@ -155,16 +188,24 @@
 
     group_count = eighths // group_rows
 
-    def build(place, most):
+    zero = jnp.zeros((8, 128), jnp.float32)
+    none = jnp.zeros((8, 128), jnp.int32)
+
+    def partition_from(place):
         pair = (place + 1) // 2
         step = jnp.where(pair % 2 == 1, (pair + 1) // 2, chips - pair // 2)
         step = jnp.where(pair == 0, 0, step)
-        wanted = ((chip + step) % chips) * 2 + (core + (place + 1) % 2) % 2
+        return ((chip + step) % chips) * 2 + (core + (place + 1) % 2) % 2
+
+    def build(place, carry):
+        most, left, codes, values = carry
+        codes, values = list(codes), list(values)
+        wanted = partition_from(place)
         for group in range(group_count):
-            seen = jnp.zeros((8, 128), jnp.int32)
-            lanes = [jnp.zeros((8, 128), jnp.int32)] * rounds_of
+            seen = none
+            lanes = [none] * rounds_of
             for g in range(group * group_rows, (group + 1) * group_rows):
-                shares = [jnp.zeros((8, 128), jnp.float32)] * rounds_of
+                shares = [zero] * rounds_of
                 for k in range(DEG):
                     entry = edge[k, g]
                     value = weight[k, g]
@@ -176,15 +217,47 @@
                         lanes[r] = jnp.where(take, slot, lanes[r])
                         shares[r] = jnp.where(take, value, shares[r])
                     seen = jnp.where(match, seen + 1, seen)
+                    if spare:
+                        over = number >= rounds_of
+                        number = jnp.where(over, left, -1)
+                        for q in range(spare):
+                            take = number == q
+                            codes[q] = jnp.where(take, entry + g * width, codes[q])
+                            values[q] = jnp.where(take, value, values[q])
+                        left = jnp.where(over, left + 1, left)
                 for r in range(rounds_of):
                     halo_weight[place, r, g] = shares[r]
             for r in range(rounds_of):
                 halo_lane[place, r, group] = lanes[r]
             most = jnp.maximum(most, seen)
-        return most
-
-    most = lax.fori_loop(0, count, build, jnp.zeros((8, 128), jnp.int32))
-    flag_out[...] = jnp.where(most > rounds_of, 1.0, 0.0)
+        return most, left, tuple(codes), tuple(values)
+
+    width = parts * HMAX
+    most, left, codes, values = lax.fori_loop(
+        0, count, build, (none, none, (none - 1,) * spare, (zero,) * spare)
+    )
+    if spare:
+        before = none
+        running = left
+        for row_shift in (1, 2, 4):
+            running = running + jnp.where(row >= row_shift, pltpu.roll(running, row_shift, 0), 0)
+        before = running - left
+        lane_total = block(jnp.max(running, axis=0, keepdims=True))
+        bad = (left > spare) | (lane_total > spare)
+        for slot in range(spare):
+            chosen = none - 1
+            amounts = [zero] * eighths
+            for q in range(spare):
+                take = (left > q) & (before + q == slot)
+                chosen = jnp.where(take, codes[q] % width, chosen)
+                for g in range(eighths):
+                    amounts[g] = jnp.where(take & (codes[q] // width == g), values[q], amounts[g])
+            extra_code[slot] = block(jnp.max(chosen, axis=0, keepdims=True))
+            for g in range(eighths):
+                extra_weight[slot, g] = amounts[g]
+    else:
+        bad = most > rounds_of
+    flag_out[...] = jnp.where(bad, 1.0, 0.0)
     for place in reversed(range(count)):
         pltpu.make_async_remote_copy(
             src_ref=flag_out, dst_ref=flag_in.at[inverse[place]], send_sem=sem_flag.at[0], recv_sem=sem_flag.at[1],
@@ -194,34 +267,36 @@
     def wait(ref, sem):
         pltpu.make_async_copy(ref, ref, sem).wait()
 
+    loads[5].wait()
+    loads[6].wait()
     wait(have_s.at[pl.ds(0, slabs - 1)], sem_s.at[1])
     levels = slabs * 8
-    modes = [full_product(l2m_ref[...], have_s[:, piece].reshape(levels, 128)) for piece in range(share)]
-    table = have_s[:, share].reshape(levels, 128)
-    stages = ((0, 1), (1, 2), (2, TERMS))
-    for stage, (low, high) in enumerate(stages):
-        for term in range(low, high):
-            scale = table[:, TERMS - 1 - term : TERMS - term]
-            for piece in range(share):
-                mixed = full_product(m2l_ref[...], modes[piece] * scale)
-                for peer in range(slabs):
-                    give_g[peer, term, piece] = mixed[peer * 8 : peer * 8 + 8]
-        for step in order:
+    for piece in range(share):
+        modes_ref[piece] = full_product(l2m_ref[...], have_s[:, piece].reshape(levels, 128))
+    table_ref[...] = have_s[:, share].reshape(levels, 128)
+    column = lax.broadcasted_iota(jnp.int32, (levels, 128), 1)
+
+    def mix_and_send(term):
+        scale = jnp.sum(jnp.where(column == TERMS - 1 - term, table_ref[...], 0.0), axis=1, keepdims=True)
+        for piece in range(share):
+            mixed = full_product(m2l_ref[...], modes_ref[piece] * scale)
+            for peer in range(slabs):
+                give_g[peer, term, piece] = mixed[peer * 8 : peer * 8 + 8]
+        for step in order2:
             peer = (slab + step) % slabs
             pltpu.make_async_remote_copy(
-                src_ref=give_g.at[peer, pl.ds(low, high - low)],
-                dst_ref=have_g.at[pl.ds(low, high - low), slab],
-                send_sem=sem_g.at[0, stage], recv_sem=sem_g.at[1, stage],
+                src_ref=give_g.at[peer, term], dst_ref=have_g.at[term, slab],
+                send_sem=sem_g.at[0, term], recv_sem=sem_g.at[1, term],
                 device_id={"lev": peer}, device_id_type=MESH,
             ).start()
-        for term in range(low, high):
-            have_g[term, slab] = give_g[slab, term]
-
-    def wait_stage(stage):
-        low, high = stages[stage]
-        wait(have_g.at[pl.ds(low, high - low), pl.ds(0, slabs - 1)], sem_g.at[1, stage])
-
-    wait_stage(0)
+        have_g[term, slab] = give_g[slab, term]
+
+    def wait_term(term, way):
+        wait(have_g.at[term, pl.ds(0, slabs - 1)], sem_g.at[way, term])
+
+    mix_and_send(0)
+    mix_and_send(1)
+    wait_term(0, 1)
     for tile in range(tiles):
         field[0, tile] = have_g[0, tile // share, tile % share]
         field[1, tile] = jnp.zeros((8, 128), jnp.float32)
@@ -237,20 +312,25 @@
         def _():
             wait(send.at[now], sem_send.at[now])
 
-        for place in reversed(range(count)):
-            code = pack[place]
-            lanes = code & 127
-            found = [lane_gather(field[now, tile], lanes) for tile in range(tiles)]
-            for bit in range(bits):
-                odd = (code & (128 << bit)) != 0
-                found = [jnp.where(odd, found[2 * i + 1], found[2 * i]) for i in range(len(found) // 2)]
-            send[now, place] = found[0]
-            group = [i for i, (low, high) in enumerate(groups) if low <= inverse[place] < high][0]
-            pltpu.make_async_remote_copy(
-                src_ref=send.at[now, place], dst_ref=halo.at[now, inverse[place]],
-                send_sem=sem_send.at[now], recv_sem=sem_recv.at[now, group],
-                device_id={"cells": partition_at(place)}, device_id_type=MESH,
-            ).start()
+        for low, high in reversed(groups):
+            for place in range(low, high):
+                code = pack[place]
+                lanes = code & 127
+                found = [lane_gather(field[now, tile], lanes) for tile in range(tiles)]
+                for bit in range(bits):
+                    odd = (code & (128 << bit)) != 0
+                    found = [jnp.where(odd, found[2 * i + 1], found[2 * i]) for i in range(len(found) // 2)]
+                send[now, place] = found[0]
+            for place in range(low, high):
+                pltpu.make_async_remote_copy(
+                    src_ref=send.at[now, place], dst_ref=halo.at[now, inverse[place]],
+                    send_sem=sem_send.at[now], recv_sem=sem_recv.at[now, groups.index((low, high))],
+                    device_id={"cells": partition_at(place)}, device_id_type=MESH,
+                ).start()
+
+        @pl.when(turn + 2 < TERMS)
+        def _():
+            mix_and_send(turn + 2)
 
         for tile in range(tiles):
             g, t = tile // 8, tile % 8
@@ -265,15 +345,24 @@
 
         @pl.when(turn == 0)
         def _():
-            wait_stage(1)
-
-        @pl.when(turn == 1)
-        def _():
-            wait_stage(2)
-
+            wait(flag_in, sem_flag.at[0])
+            wait(flag_in, sem_flag.at[1])
+            worst = flag_out[...]
+            for place in range(count):
+                worst = jnp.maximum(worst, flag_in[place])
+            flag_ref[0, 0] = jnp.max(worst).astype(jnp.int32)
+
+        wait_term(turn + 1, 1)
         scale = jnp.where(turn == TERMS - 2, 0.5, 1.0)
+        extras = [zero] * spare
         for index, (low, high) in enumerate(groups):
             wait(halo.at[now, pl.ds(low, high - low)], sem_recv.at[now, index])
+            last_group = index == len(groups) - 1
+            for place in range(low, high):
+                for slot in range(spare):
+                    code = extra_code[slot]
+                    got = lane_gather(halo[now, place], code & 127)
+                    extras[slot] = jnp.where((code >> 7) == partition_at(place), got, extras[slot])
             for t in range(8):
                 for group in range(group_count):
                     rows = range(group * group_rows, (group + 1) * group_rows)
@@ -287,9 +376,11 @@
                                 values[i] = values[i] + block(halo_weight[place, r, g, t : t + 1, :]) * got
                     for i, g in enumerate(rows):
                         tile = 8 * g + t
-                        if index < len(groups) - 1:
+                        if not last_group:
                             total[tile] = values[i]
                         else:
+                            for slot in range(spare):
+                                values[i] = values[i] + block(extra_weight[slot, g, t : t + 1, :]) * extras[slot]
                             field[old, tile] = (
                                 have_g[turn + 1, tile // share, tile % share] + scale * values[i] - field[old, tile]
                             )
@@ -304,17 +395,11 @@
     for now in range(2):
         wait(send.at[now], sem_send.at[now])
     wait(give_s.at[pl.ds(0, slabs - 1)], sem_s.at[0])
-    for stage, (low, high) in enumerate(stages):
-        wait(have_g.at[pl.ds(low, high - low), pl.ds(0, slabs - 1)], sem_g.at[0, stage])
-    wait(flag_in, sem_flag.at[0])
-    wait(flag_in, sem_flag.at[1])
-    worst = flag_out[...]
-    for place in range(count):
-        worst = jnp.maximum(worst, flag_in[place])
-    flag_ref[...] = worst
-
-
-def solve(parts, slabs, group_rows, rounds_of, number, source, l2m, m2l, shift, weights, near, lists):
+    for term in range(TERMS):
+        wait_term(term, 0)
+
+
+def solve(parts, slabs, group_rows, rounds_of, spare, number, source, l2m, m2l, shift, weights, near, lists):
     columns = source.shape[1]
     tiles = columns // 128
     eighths = tiles // 8
@@ -322,17 +407,24 @@
     peers = parts - 1
     f32, i32 = jnp.float32, jnp.int32
     groups = len(peers_of(parts // 2)[1])
-    vmem = pl.BlockSpec(memory_space=pltpu.VMEM)
+    slots = max(spare, 1)
     return pl.pallas_call(
-        functools.partial(kernel, parts, slabs, group_rows, rounds_of),
+        functools.partial(kernel, parts, slabs, group_rows, rounds_of, spare),
         name=f"solve_{number}",
         out_shape=(
             jax.ShapeDtypeStruct(source.shape, f32),
-            jax.ShapeDtypeStruct((8, 128), f32),
+            jax.ShapeDtypeStruct((1, 1), i32),
         ),
-        in_specs=[pl.BlockSpec(memory_space=pltpu.SMEM)] + [vmem] * 6,
-        out_specs=(vmem, vmem),
+        in_specs=[pl.BlockSpec(memory_space=pltpu.HBM)] * 7,
+        out_specs=(pl.BlockSpec(memory_space=pltpu.VMEM), pl.BlockSpec(memory_space=pltpu.SMEM)),
         scratch_shapes=[
+            pltpu.VMEM(shift.shape, f32),
+            pltpu.VMEM(source.shape, f32),
+            pltpu.VMEM(l2m.shape, f32),
+            pltpu.VMEM(m2l.shape, f32),
+            pltpu.VMEM(weights.shape, f32),
+            pltpu.VMEM(near.shape, i32),
+            pltpu.VMEM(lists.shape, i32),
             pltpu.VMEM((DEG, eighths, 8, 128), i32),
             pltpu.VMEM((DEG, eighths, 8, 128), f32),
             pltpu.VMEM((DEG, eighths, 8, 128), i32),
@@ -341,9 +433,13 @@
             pltpu.VMEM((eighths, 8, 128), f32),
             pltpu.VMEM((peers, rounds_of, eighths // group_rows, 8, 128), i32),
             pltpu.VMEM((peers, rounds_of, eighths, 8, 128), f32),
+            pltpu.VMEM((slots, 8, 128), i32),
+            pltpu.VMEM((slots, eighths, 8, 128), f32),
             pltpu.VMEM((peers, 8, 128), i32),
             pltpu.VMEM((slabs, share + 1, 8, 128), f32),
             pltpu.VMEM((slabs, share + 1, 8, 128), f32),
+            pltpu.VMEM((share, l2m.shape[0], 128), f32),
+            pltpu.VMEM((l2m.shape[0], 128), f32),
             pltpu.VMEM((slabs, TERMS, share, 8, 128), f32),
             pltpu.VMEM((TERMS, slabs, share, 8, 128), f32),
             pltpu.VMEM((2, tiles, 8, 128), f32),
@@ -352,8 +448,9 @@
             pltpu.VMEM((2, peers, 8, 128), f32),
             pltpu.VMEM((8, 128), f32),
             pltpu.VMEM((peers, 8, 128), f32),
+            pltpu.SemaphoreType.DMA((7,)),
             pltpu.SemaphoreType.DMA((2,)),
-            pltpu.SemaphoreType.DMA((2, 3)),
+            pltpu.SemaphoreType.DMA((2, TERMS)),
             pltpu.SemaphoreType.DMA((2,)),
             pltpu.SemaphoreType.DMA((2, groups)),
             pltpu.SemaphoreType.DMA((2,)),
@@ -364,8 +461,8 @@
     )(shift, source, l2m, m2l, weights, near, lists)
 
 
-FAST = (4, 5)
-SAFE = (1, DEG)
+FAST = (4, 2, 3)
+SAFE = (1, DEG, 0)
 
 
 def solution(mesh):
@@ -374,12 +471,14 @@
     def local(source, l2m, m2l, shift, weights, near, lists):
         arrays = (source, l2m, m2l, shift, weights, near, lists)
         eighths = source.shape[1] // 1024
-        fast = (min(FAST[0], eighths), FAST[1])
+        fast = (min(FAST[0], eighths), *FAST[1:])
         answer, flag = solve(parts, slabs, *fast, 0, *arrays)
-        return lax.cond(
-            flag[0, 0] > 0.0,
-            lambda arrays, answer: solve(parts, slabs, *SAFE, 1, *arrays)[0],
-            lambda arrays, answer: answer,
+        return lax.switch(
+            flag[0, 0],
+            (
+                lambda arrays, answer: answer,
+                lambda arrays, answer: solve(parts, slabs, *SAFE, 1, *arrays)[0],
+            ),
             arrays,
             answer,
         )

time: 72.9 us -> 62 us (0.85)
  Pallas kernels: 70 us -> 59.6 us
    pallas_call x1, Pallas kernels: 70 us -> 59.6 us  [solve(): pl.pallas_call(functools.partial(kernel, parts, slabs, group_rows, rounds...]
where the time goes in v2:
time: 62 us; the launch traced here: 61.9 us
  Pallas kernels  59.6 us (96%)
  local copies, waits for them, and re-layouts  1.34 us (2%)
  between operations  0.72 us (1%)
    pallas_call x1, Pallas kernels, solve(): pl.pallas_call(functools.partial(kernel, parts, slabs, group_rows, rounds...  59.6 us
    unnamed x15, local copies, waits for them, and re-layouts  1.34 us

profile of v2, /device:TPU:1, one launch (start us, length us, event | category | flops | bytes accessed | tf_op | source)
XLA Modules:
  0.0 61.9 jit_solution(16438521423045581843)
XLA Ops:
  0.0 0.0 copy-start.6
  0.0 0.7 %copy-done.6 = f32[8]{0:T(128)S(1)} copy-done((f32[8]{0:T(128)S(1)}, f32[8]{0:T(128)}, u32[]{:S(2)}) %copy-start.6) | copy-done | bytes 56
  0.7 0.0 copy-start
  0.7 0.0 copy-start.1
  0.7 0.0 copy-start.2
  0.7 0.0 copy-start.3
  0.7 0.0 copy-start.4
  0.7 0.0 copy-start.5
  0.7 59.6 %solve_0.1 = (f32[8,4096]{1,0:T(8,128)S(1)}, s32[1,1]{1,0:T(1,128)}) custom-call(f32[8]{0:T(128)S(1)} %copy-done.6, f32[8,4096]{1,0:T(8,128)} %source_hbm.1, f32[128,128]{1,0:T(8,128)} %l2m_hbm.1, f32[128,128]{1,0:T(8,128)} %m2l_hbm.1, f32[6,4096]{1,0:T(8,128)} %weight_hbm.1, s32[6,4096]{1,0:T(8,128)} %near_hbm.1, s32[1,2048]{1,0:T(1,128)} %list_hbm.1), custom_call_target="tpu_custom_call" | custom-call | tf_op jit(solution)/shard_map/solve_0/pallas_call | solution.py:411
  60.9 0.0 copy-done
  61.0 0.0 copy-done.1
  61.0 0.0 copy-done.2
  61.0 0.0 copy-done.3
  61.0 0.0 copy-done.4
  61.0 0.0 copy-done.5
  61.0 0.2 conditional.1
  61.2 0.7 %copy.13 = f32[8,4096]{1,0:T(8,128)} copy(f32[8,4096]{1,0:T(8,128)S(1)} %get-tuple-element.35) | data formatting | bytes 262144
Async XLA Ops:
  0.0 0.7 %copy-start.6 = (f32[8]{0:T(128)S(1)}, f32[8]{0:T(128)}, u32[]{:S(2)}) copy-start(f32[8]{0:T(128)} %shift_hbm.1) | copy-start | bytes 100
  0.7 60.3 %copy-start = (f32[8,4096]{1,0:T(8,128)S(1)}, f32[8,4096]{1,0:T(8,128)}, u32[]{:S(2)}) copy-start(f32[8,4096]{1,0:T(8,128)} %source_hbm.1) | copy-start | bytes 393220
  0.7 60.3 %copy-start.1 = (f32[6,4096]{1,0:T(8,128)S(1)}, f32[6,4096]{1,0:T(8,128)}, u32[]{:S(2)}) copy-start(f32[6,4096]{1,0:T(8,128)} %weight_hbm.1) | copy-start | bytes 294916
  0.7 60.3 %copy-start.2 = (s32[6,4096]{1,0:T(8,128)S(1)}, s32[6,4096]{1,0:T(8,128)}, u32[]{:S(2)}) copy-start(s32[6,4096]{1,0:T(8,128)} %near_hbm.1) | copy-start | bytes 294916
  0.7 60.3 %copy-start.3 = (f32[128,128]{1,0:T(8,128)S(1)}, f32[128,128]{1,0:T(8,128)}, u32[]{:S(2)}) copy-start(f32[128,128]{1,0:T(8,128)} %l2m_hbm.1) | copy-start | bytes 196612
  0.7 60.3 %copy-start.4 = (f32[128,128]{1,0:T(8,128)S(1)}, f32[128,128]{1,0:T(8,128)}, u32[]{:S(2)}) copy-start(f32[128,128]{1,0:T(8,128)} %m2l_hbm.1) | copy-start | bytes 196612
  0.7 60.3 %copy-start.5 = (s32[1,2048]{1,0:T(1,128)S(1)}, s32[1,2048]{1,0:T(1,128)}, u32[]{:S(2)}) copy-start(s32[1,2048]{1,0:T(1,128)} %list_hbm.1) | copy-start | bytes 24580

commit v3 on v2

--- a/solution.py
+++ b/solution.py
@@ -312,11 +312,13 @@
         def _():
             wait(send.at[now], sem_send.at[now])
 
+        whole = [field[now, tile] for tile in range(tiles)]
+        codes = [pack[place] for place in range(count)]
         for low, high in reversed(groups):
             for place in range(low, high):
-                code = pack[place]
+                code = codes[place]
                 lanes = code & 127
-                found = [lane_gather(field[now, tile], lanes) for tile in range(tiles)]
+                found = [lane_gather(whole[tile], lanes) for tile in range(tiles)]
                 for bit in range(bits):
                     odd = (code & (128 << bit)) != 0
                     found = [jnp.where(odd, found[2 * i + 1], found[2 * i]) for i in range(len(found) // 2)]

time: 62 us -> 60.7 us (0.979)
  Pallas kernels: 59.6 us -> 58.3 us
    pallas_call x1, Pallas kernels: 59.6 us -> 58.3 us  [solve(): pl.pallas_call(functools.partial(kernel, parts, slabs, group_rows, rounds...]
where the time goes in v3:
time: 60.7 us; the launch traced here: 60.6 us
  Pallas kernels  58.3 us (96%)
  local copies, waits for them, and re-layouts  1.34 us (2%)
  between operations  0.72 us (1%)
    pallas_call x1, Pallas kernels, solve(): pl.pallas_call(functools.partial(kernel, parts, slabs, group_rows, rounds...  58.3 us
    unnamed x15, local copies, waits for them, and re-layouts  1.34 us

profile of v3, /device:TPU:1, one launch (start us, length us, event | category | flops | bytes accessed | tf_op | source)
XLA Modules:
  0.0 60.6 jit_solution(3637100286265524579)
XLA Ops:
  0.0 0.0 copy-start.6
  0.0 0.7 %copy-done.6 = f32[8]{0:T(128)S(1)} copy-done((f32[8]{0:T(128)S(1)}, f32[8]{0:T(128)}, u32[]{:S(2)}) %copy-start.6) | copy-done | bytes 56
  0.7 0.0 copy-start
  0.7 0.0 copy-start.1
  0.7 0.0 copy-start.2
  0.7 0.0 copy-start.3
  0.7 0.0 copy-start.4
  0.7 0.0 copy-start.5
  0.7 58.3 %solve_0.1 = (f32[8,4096]{1,0:T(8,128)S(1)}, s32[1,1]{1,0:T(1,128)}) custom-call(f32[8]{0:T(128)S(1)} %copy-done.6, f32[8,4096]{1,0:T(8,128)} %source_hbm.1, f32[128,128]{1,0:T(8,128)} %l2m_hbm.1, f32[128,128]{1,0:T(8,128)} %m2l_hbm.1, f32[6,4096]{1,0:T(8,128)} %weight_hbm.1, s32[6,4096]{1,0:T(8,128)} %near_hbm.1, s32[1,2048]{1,0:T(1,128)} %list_hbm.1), custom_call_target="tpu_custom_call" | custom-call | tf_op jit(solution)/shard_map/solve_0/pallas_call | solution.py:413
  59.7 0.0 copy-done
  59.7 0.0 copy-done.1
  59.7 0.0 copy-done.2
  59.7 0.0 copy-done.3
  59.7 0.0 copy-done.4
  59.7 0.0 copy-done.5
  59.7 0.2 conditional.1
  59.9 0.7 %copy.13 = f32[8,4096]{1,0:T(8,128)} copy(f32[8,4096]{1,0:T(8,128)S(1)} %get-tuple-element.35) | data formatting | bytes 262144
Async XLA Ops:
  0.0 0.7 %copy-start.6 = (f32[8]{0:T(128)S(1)}, f32[8]{0:T(128)}, u32[]{:S(2)}) copy-start(f32[8]{0:T(128)} %shift_hbm.1) | copy-start | bytes 100
  0.7 59.0 %copy-start = (f32[8,4096]{1,0:T(8,128)S(1)}, f32[8,4096]{1,0:T(8,128)}, u32[]{:S(2)}) copy-start(f32[8,4096]{1,0:T(8,128)} %source_hbm.1) | copy-start | bytes 393220
  0.7 59.0 %copy-start.1 = (f32[6,4096]{1,0:T(8,128)S(1)}, f32[6,4096]{1,0:T(8,128)}, u32[]{:S(2)}) copy-start(f32[6,4096]{1,0:T(8,128)} %weight_hbm.1) | copy-start | bytes 294916
  0.7 59.0 %copy-start.2 = (s32[6,4096]{1,0:T(8,128)S(1)}, s32[6,4096]{1,0:T(8,128)}, u32[]{:S(2)}) copy-start(s32[6,4096]{1,0:T(8,128)} %near_hbm.1) | copy-start | bytes 294916
  0.7 59.0 %copy-start.3 = (f32[128,128]{1,0:T(8,128)S(1)}, f32[128,128]{1,0:T(8,128)}, u32[]{:S(2)}) copy-start(f32[128,128]{1,0:T(8,128)} %l2m_hbm.1) | copy-start | bytes 196612
  0.7 59.0 %copy-start.4 = (f32[128,128]{1,0:T(8,128)S(1)}, f32[128,128]{1,0:T(8,128)}, u32[]{:S(2)}) copy-start(f32[128,128]{1,0:T(8,128)} %m2l_hbm.1) | copy-start | bytes 196612
  0.7 59.0 %copy-start.5 = (s32[1,2048]{1,0:T(1,128)S(1)}, s32[1,2048]{1,0:T(1,128)}, u32[]{:S(2)}) copy-start(s32[1,2048]{1,0:T(1,128)} %list_hbm.1) | copy-start | bytes 24580

commit v4 on v3

--- a/solution.py
+++ b/solution.py
@@ -157,7 +157,15 @@
     for step in order:
         peer = (slab + step) % slabs
         pltpu.make_async_remote_copy(
-            src_ref=give_s.at[peer], dst_ref=have_s.at[slab], send_sem=sem_s.at[0], recv_sem=sem_s.at[1],
+            src_ref=give_s.at[peer, pl.ds(0, share)], dst_ref=have_s.at[slab, pl.ds(0, share)],
+            send_sem=sem_s.at[0], recv_sem=sem_s.at[1],
+            device_id={"lev": peer}, device_id_type=MESH,
+        ).start()
+    for step in order:
+        peer = (slab + step) % slabs
+        pltpu.make_async_remote_copy(
+            src_ref=give_s.at[peer, share], dst_ref=have_s.at[slab, share],
+            send_sem=sem_s.at[2], recv_sem=sem_s.at[3],
             device_id={"lev": peer}, device_id_type=MESH,
         ).start()
 
@@ -269,10 +277,11 @@
 
     loads[5].wait()
     loads[6].wait()
-    wait(have_s.at[pl.ds(0, slabs - 1)], sem_s.at[1])
+    wait(have_s.at[pl.ds(0, slabs - 1), pl.ds(0, share)], sem_s.at[1])
     levels = slabs * 8
     for piece in range(share):
         modes_ref[piece] = full_product(l2m_ref[...], have_s[:, piece].reshape(levels, 128))
+    wait(have_s.at[pl.ds(0, slabs - 1), share], sem_s.at[3])
     table_ref[...] = have_s[:, share].reshape(levels, 128)
     column = lax.broadcasted_iota(jnp.int32, (levels, 128), 1)
 
@@ -396,7 +405,8 @@
 
     for now in range(2):
         wait(send.at[now], sem_send.at[now])
-    wait(give_s.at[pl.ds(0, slabs - 1)], sem_s.at[0])
+    wait(give_s.at[pl.ds(0, slabs - 1), pl.ds(0, share)], sem_s.at[0])
+    wait(give_s.at[pl.ds(0, slabs - 1), share], sem_s.at[2])
     for term in range(TERMS):
         wait_term(term, 0)
 
@@ -451,7 +461,7 @@
             pltpu.VMEM((8, 128), f32),
             pltpu.VMEM((peers, 8, 128), f32),
             pltpu.SemaphoreType.DMA((7,)),
-            pltpu.SemaphoreType.DMA((2,)),
+            pltpu.SemaphoreType.DMA((4,)),
             pltpu.SemaphoreType.DMA((2, TERMS)),
             pltpu.SemaphoreType.DMA((2,)),
             pltpu.SemaphoreType.DMA((2, groups)),

time: 60.7 us -> 61.3 us (level)
  no operation moved by 1% of the time
where the time goes in v4:
time: 61.3 us; the launch traced here: 61.1 us
  Pallas kernels  58.9 us (96%)
  local copies, waits for them, and re-layouts  1.34 us (2%)
  between operations  0.72 us (1%)
    pallas_call x1, Pallas kernels, solve(): pl.pallas_call(functools.partial(kernel, parts, slabs, group_rows, rounds...  58.9 us
    unnamed x15, local copies, waits for them, and re-layouts  1.34 us

profile of v4, /device:TPU:1, one launch (start us, length us, event | category | flops | bytes accessed | tf_op | source)
XLA Modules:
  0.0 61.1 jit_solution(1491065477161936344)
XLA Ops:
  0.0 0.0 copy-start.6
  0.0 0.7 %copy-done.6 = f32[8]{0:T(128)S(1)} copy-done((f32[8]{0:T(128)S(1)}, f32[8]{0:T(128)}, u32[]{:S(2)}) %copy-start.6) | copy-done | bytes 56
  0.7 0.0 copy-start
  0.7 0.0 copy-start.1
  0.7 0.0 copy-start.2
  0.7 0.0 copy-start.3
  0.7 0.0 copy-start.4
  0.7 0.0 copy-start.5
  0.7 58.9 %solve_0.1 = (f32[8,4096]{1,0:T(8,128)S(1)}, s32[1,1]{1,0:T(1,128)}) custom-call(f32[8]{0:T(128)S(1)} %copy-done.6, f32[8,4096]{1,0:T(8,128)} %source_hbm.1, f32[128,128]{1,0:T(8,128)} %l2m_hbm.1, f32[128,128]{1,0:T(8,128)} %m2l_hbm.1, f32[6,4096]{1,0:T(8,128)} %weight_hbm.1, s32[6,4096]{1,0:T(8,128)} %near_hbm.1, s32[1,2048]{1,0:T(1,128)} %list_hbm.1), custom_call_target="tpu_custom_call" | custom-call | tf_op jit(solution)/shard_map/solve_0/pallas_call | solution.py:423
  60.2 0.0 copy-done
  60.2 0.0 copy-done.1
  60.2 0.0 copy-done.2
  60.3 0.0 copy-done.3
  60.3 0.0 copy-done.4
  60.3 0.0 copy-done.5
  60.3 0.2 conditional.1
  60.5 0.7 %copy.13 = f32[8,4096]{1,0:T(8,128)} copy(f32[8,4096]{1,0:T(8,128)S(1)} %get-tuple-element.35) | data formatting | bytes 262144
Async XLA Ops:
  0.0 0.7 %copy-start.6 = (f32[8]{0:T(128)S(1)}, f32[8]{0:T(128)}, u32[]{:S(2)}) copy-start(f32[8]{0:T(128)} %shift_hbm.1) | copy-start | bytes 100
  0.7 59.6 %copy-start = (f32[8,4096]{1,0:T(8,128)S(1)}, f32[8,4096]{1,0:T(8,128)}, u32[]{:S(2)}) copy-start(f32[8,4096]{1,0:T(8,128)} %source_hbm.1) | copy-start | bytes 393220
  0.7 59.6 %copy-start.1 = (f32[6,4096]{1,0:T(8,128)S(1)}, f32[6,4096]{1,0:T(8,128)}, u32[]{:S(2)}) copy-start(f32[6,4096]{1,0:T(8,128)} %weight_hbm.1) | copy-start | bytes 294916
  0.7 59.6 %copy-start.2 = (s32[6,4096]{1,0:T(8,128)S(1)}, s32[6,4096]{1,0:T(8,128)}, u32[]{:S(2)}) copy-start(s32[6,4096]{1,0:T(8,128)} %near_hbm.1) | copy-start | bytes 294916
  0.7 59.6 %copy-start.3 = (f32[128,128]{1,0:T(8,128)S(1)}, f32[128,128]{1,0:T(8,128)}, u32[]{:S(2)}) copy-start(f32[128,128]{1,0:T(8,128)} %l2m_hbm.1) | copy-start | bytes 196612
  0.7 59.6 %copy-start.4 = (f32[128,128]{1,0:T(8,128)S(1)}, f32[128,128]{1,0:T(8,128)}, u32[]{:S(2)}) copy-start(f32[128,128]{1,0:T(8,128)} %m2l_hbm.1) | copy-start | bytes 196612
  0.7 59.6 %copy-start.5 = (s32[1,2048]{1,0:T(1,128)S(1)}, s32[1,2048]{1,0:T(1,128)}, u32[]{:S(2)}) copy-start(s32[1,2048]{1,0:T(1,128)} %list_hbm.1) | copy-start | bytes 24580
